TPU v7x, 256 devices: a whole 4x4x8 slice. The times are simulated.
256 devices in a mesh: seq: 32 (over x_lo, z, core), tp: 8 (over y, x_hi).
Axes of the slice: x: 4 (x_hi: 2, x_lo: 2; x = x_hi * 2 + x_lo), y: 4, z: 8, core: 2. Of those that a mesh axis runs over, the one named last changes fastest.
Arguments:
- values: bfloat16 [8192, 4096], P('seq', 'tp'), may hold values from -6 to 6
- gate: bfloat16 [8192, 4096], P('seq', 'tp'), may hold values from -6 to 6
- out_grad: bfloat16 [8192, 4096], P('seq', 'tp'), may hold values from -6 to 6
- out_weight: bfloat16 [4096, 4096], P(None, 'tp'), may hold values from -0.09375 to 0.09375
- filt: float32 [8192, 4096], P('seq', 'tp'), may hold values from -6 to 6
- decay: float32 [4096], P('tp'), may hold values from 0.5 to 16
Outputs:
- d_values: bfloat16 [8192, 4096], P('seq', 'tp')
- d_gate: bfloat16 [8192, 4096], P('seq', 'tp')
- d_filt: float32 [8192, 4096], P('seq', 'tp')
- decay_grad: float32 [4096], P('tp')
- d_out_weight: float32 [4096, 4096], P('seq', 'tp')
All inputs are finite; a program needn't handle non-finite values.
Results may differ from a plain program's by a relative error of at most 0.0085.
Values may be sent and summed in bfloat16 or wider, within the bound.
A program may use at most 128 MiB of HBM per device.

v0:
```python
import math
import jax
import jax.numpy as jnp
from jax import lax
from jax.sharding import PartitionSpec as P

HIGHEST = lax.Precision.HIGHEST
TWO_PI = 2.0 * math.pi


def angles(left_idx, right_idx, modulus):
    index = left_idx[:, None] * right_idx[None, :] % modulus
    phase = index.astype(jnp.float32) * (TWO_PI / modulus)
    return (jnp.cos(phase), jnp.sin(phase))


def forward_outer(block, outer_cos, outer_sin, twid_cos, twid_sin):
    real_part = jnp.einsum("kp,fprc->fkrc", outer_cos, block, precision=HIGHEST)
    imag_part = -jnp.einsum("kp,fprc->fkrc", outer_sin, block, precision=HIGHEST)
    cos_b = twid_cos[None, :, :, None]
    sin_b = twid_sin[None, :, :, None]
    return jnp.stack([real_part * cos_b + imag_part * sin_b, imag_part * cos_b - real_part * sin_b])


def forward_inner(block, inner_cos, inner_sin):
    shape = block.shape
    merged = block.reshape(shape[0], shape[1], shape[2], shape[3] * shape[4], shape[5])
    real_in = merged[0]
    imag_in = merged[1]
    real_out = jnp.einsum("kb,fjbc->fjkc", inner_cos, real_in, precision=HIGHEST) + jnp.einsum(
        "kb,fjbc->fjkc", inner_sin, imag_in, precision=HIGHEST
    )
    imag_out = jnp.einsum("kb,fjbc->fjkc", inner_cos, imag_in, precision=HIGHEST) - jnp.einsum(
        "kb,fjbc->fjkc", inner_sin, real_in, precision=HIGHEST
    )
    return jnp.stack([real_out, imag_out])


def products(spectrum):
    real_v, real_k, real_g = (spectrum[0, 0], spectrum[0, 1], spectrum[0, 2])
    imag_v, imag_k, imag_g = (spectrum[1, 0], spectrum[1, 1], spectrum[1, 2])
    real_out = jnp.stack(
        [
            real_v * real_k - imag_v * imag_k,
            real_k * real_g + imag_k * imag_g,
            real_v * real_g + imag_v * imag_g,
        ]
    )
    imag_out = jnp.stack(
        [
            real_v * imag_k + imag_v * real_k,
            real_k * imag_g - imag_k * real_g,
            real_v * imag_g - imag_v * real_g,
        ]
    )
    return jnp.stack([real_out, imag_out])


def inverse_inner(spectrum, inner_cos, inner_sin, twid_cos, twid_sin):
    real_in = spectrum[0]
    imag_in = spectrum[1]
    real_mid = jnp.einsum("bk,fjkc->fjbc", inner_cos, real_in, precision=HIGHEST) - jnp.einsum(
        "bk,fjkc->fjbc", inner_sin, imag_in, precision=HIGHEST
    )
    imag_mid = jnp.einsum("bk,fjkc->fjbc", inner_cos, imag_in, precision=HIGHEST) + jnp.einsum(
        "bk,fjkc->fjbc", inner_sin, real_in, precision=HIGHEST
    )
    cos_b = twid_cos[None, :, :, None]
    sin_b = twid_sin[None, :, :, None]
    return jnp.stack([real_mid * cos_b - imag_mid * sin_b, real_mid * sin_b + imag_mid * cos_b])


def inverse_outer(block, back_cos, back_sin, padded):
    shape = block.shape
    merged = block.reshape(shape[0], shape[1], shape[2] * shape[3], shape[4], shape[5])
    result = jnp.einsum("pk,fkrc->fprc", back_cos, merged[0], precision=HIGHEST) - jnp.einsum(
        "pk,fkrc->fprc", back_sin, merged[1], precision=HIGHEST
    )
    return result / padded


def home_inputs(gate, grad_y, filt, decay, my_index, tok_rows, length, norm_scale):
    position = (
        (my_index * tok_rows + jnp.arange(tok_rows, dtype=jnp.int32)).astype(jnp.float32) / length
    )[:, None]
    window = jnp.exp(-decay[None, :] * position)
    kernel = filt * window * norm_scale
    gated_grad = grad_y.astype(jnp.float32) * gate.astype(jnp.float32)
    return (position, window, kernel, gated_grad)


def home_results(
    conv_out, conv_grad, kernel_grad, gate, grad_y, position, window, kernel, norm_scale
):
    d_values = conv_grad.astype(jnp.bfloat16)
    d_gate = (grad_y.astype(jnp.float32) * conv_out).astype(jnp.bfloat16)
    gated_out = (gate.astype(jnp.float32) * conv_out).astype(jnp.bfloat16)
    d_filt = kernel_grad * window * norm_scale
    decay_part = jnp.sum(position * kernel_grad * kernel, axis=0)
    return (d_values, d_gate, gated_out, d_filt, decay_part)


def on_device(values, gate, out_grad, out_weight, filt, decay):
    tok_rows = values.shape[0]
    seq_parts = lax.axis_size("seq")
    my_index = lax.axis_index("seq")
    sub_rows = tok_rows // seq_parts
    length = tok_rows * seq_parts
    padded = 2 * length
    norm_scale = 1.0 / math.sqrt(length)
    full_grad = lax.all_gather(out_grad, "tp", axis=1, tiled=True)
    grad_y = jnp.dot(full_grad, out_weight, preferred_element_type=jnp.float32).astype(jnp.bfloat16)
    outer_cos, outer_sin = angles(
        jnp.arange(2 * seq_parts, dtype=jnp.int32),
        jnp.arange(seq_parts, dtype=jnp.int32),
        2 * seq_parts,
    )
    back_cos, back_sin = angles(
        jnp.arange(seq_parts, dtype=jnp.int32),
        jnp.arange(2 * seq_parts, dtype=jnp.int32),
        2 * seq_parts,
    )
    inner_cos, inner_sin = angles(
        jnp.arange(tok_rows, dtype=jnp.int32), jnp.arange(tok_rows, dtype=jnp.int32), tok_rows
    )
    fwd_cos, fwd_sin = angles(
        jnp.arange(2 * seq_parts, dtype=jnp.int32),
        my_index * sub_rows + jnp.arange(sub_rows, dtype=jnp.int32),
        padded,
    )
    inv_cos, inv_sin = angles(
        2 * my_index + jnp.arange(2, dtype=jnp.int32), jnp.arange(tok_rows, dtype=jnp.int32), padded
    )
    position, window, kernel, gated_grad = home_inputs(
        gate, grad_y, filt, decay, my_index, tok_rows, length, norm_scale
    )
    fields = jnp.stack([values.astype(jnp.float32), kernel, gated_grad])[:, None]
    half_spectrum = forward_outer(
        lax.all_to_all(fields, "seq", split_axis=2, concat_axis=1, tiled=True),
        outer_cos,
        outer_sin,
        fwd_cos,
        fwd_sin,
    )
    spectrum = forward_inner(
        lax.all_to_all(
            half_spectrum[:, :, :, None], "seq", split_axis=2, concat_axis=3, tiled=True
        ),
        inner_cos,
        inner_sin,
    )
    inverted = inverse_inner(products(spectrum), inner_cos, inner_sin, inv_cos, inv_sin)
    fields_away = inverse_outer(
        lax.all_to_all(inverted[:, :, None], "seq", split_axis=4, concat_axis=2, tiled=True),
        back_cos,
        back_sin,
        padded,
    )
    returned = lax.all_to_all(fields_away, "seq", split_axis=1, concat_axis=2, tiled=True)
    d_values, d_gate, gated_out, d_filt, decay_part = home_results(
        returned[0, 0],
        returned[1, 0],
        returned[2, 0],
        gate,
        grad_y,
        position,
        window,
        kernel,
        norm_scale,
    )
    decay_grad = -norm_scale * lax.psum(decay_part, "seq")
    term = lax.dot_general(
        full_grad, gated_out, (((0,), (0,)), ((), ())), preferred_element_type=jnp.float32
    )
    d_out_weight = lax.psum_scatter(term * norm_scale, "seq", scatter_dimension=0, tiled=True)
    return (d_values, d_gate, d_filt, decay_grad, d_out_weight)


def solution(mesh):
    in_specs = (
        P("seq", "tp"),
        P("seq", "tp"),
        P("seq", "tp"),
        P(None, "tp"),
        P("seq", "tp"),
        P("tp"),
    )
    out_specs = (P("seq", "tp"), P("seq", "tp"), P("seq", "tp"), P("tp"), P("seq", "tp"))
    return jax.shard_map(
        on_device, mesh=mesh, in_specs=in_specs, out_specs=out_specs, check_vma=False
    )
```

profile of v0, /device:TPU:4, one launch (start us, length us, event | category | flops | bytes accessed | tf_op | source)
XLA Modules:
  0.0 709.1 jit_solution(6259057081510441585)
XLA Ops:
  10.8 59.6 %all-gather.2.cloned.1.call-done = bf16[256,4096]{1,0:T(8,128)(2,1)} async-done(((bf16[256,512]{1,0:T(8,128)(2,1)}), bf16[256,4096]{1,0:T(8,128)(2,1)}) %all-gather.2.cloned.1.call-update) | async-done | bytes 2097168 | tf_op jit(solution)/shard_map/all_gather | solution.py:111
  70.5 4.1 fusion.30
  78.3 9.1 %all-to-all-start = ((f32[3,1,256,512]{3,1,0,2:T(1,128)}), f32[3,1,256,512]{3,1,0,2:T(1,128)S(1)}, u32[]{:S(2)}, u32[]{:S(2)}) async-start(f32[3,1,256,512]{3,1,0,2:T(1,128)} %copy.66), calls=%async_computation | async-start | bytes 3145728 | tf_op jit(solution)/shard_map/all_to_all | solution.py:139
  87.6 38.9 %all-to-all-done = f32[3,1,256,512]{3,1,0,2:T(1,128)S(1)} async-done(((f32[3,1,256,512]{3,1,0,2:T(1,128)}), f32[3,1,256,512]{3,1,0,2:T(1,128)S(1)}, u32[]{:S(2)}, u32[]{:S(2)}) %all-to-all-start) | async-done | bytes 1572896 | tf_op jit(solution)/shard_map/all_to_all | solution.py:139
  126.6 4.0 fusion.26
  130.6 4.9 fusion.9
  136.8 6.7 copy.70
  143.5 4.9 all-to-all-start.1
  148.6 140.6 %all-to-all-done.1 = f32[2,3,64,1,8,512]{5,4,1,0,3,2:T(8,128)} async-done(((f32[2,3,64,1,8,512]{5,4,1,0,3,2:T(8,128)}), f32[2,3,64,1,8,512]{5,4,1,0,3,2:T(8,128)}, u32[]{:S(2)}, u32[]{:S(2)}) %all-to-all-start.1) | async-done | bytes 6291488 | tf_op jit(solution)/shard_map/all_to_all | solution.py:146
  294.1 6.3 fusion.2
  300.4 6.5 fusion
  306.9 6.4 add_bitcast_fusion.1
  313.3 6.7 subtract_bitcast_fusion.1
  328.3 4.3 fusion.24
  332.6 4.3 subtract_bitcast_fusion
  340.0 10.4 %copy.78 = f32[2,3,1,2,256,512]{5,3,1,0,2,4:T(2,128)} copy(f32[2,3,1,2,256,512]{4,5,3,1,0,2:T(8,128)} %maximum_bitcast_fusion.1) | data formatting | bytes 12582912 | tf_op jit(solution)/shard_map/broadcast_in_dim | solution.py:154
  350.4 148.1 %all_to_all.51 = f32[2,3,1,2,256,512]{5,3,1,0,2,4:T(2,128)S(1)} all-to-all(f32[2,3,1,2,256,512]{5,3,1,0,2,4:T(2,128)} %copy.78), channel_id=1, replica_groups=mesh['seq'=32,'tp'=8] {'seq'}, dimensions={4} | all-to-all | bytes 12582912 | tf_op jit(solution)/shard_map/all_to_all | solution.py:154
  508.7 5.2 fusion.67
  513.9 4.1 copy.81
  518.0 4.1 squeeze.28
  526.5 44.9 %all_to_all.52 = f32[3,32,8,512]{3,2,0,1:T(8,128)S(1)} all-to-all(f32[3,32,8,512]{3,2,0,1:T(8,128)S(1)} %copy.82), channel_id=1, replica_groups=mesh['seq'=32,'tp'=8] {'seq'}, dimensions={1} | all-to-all | bytes 3145728 | tf_op jit(solution)/shard_map/all_to_all | solution.py:159
  571.3 4.5 multiply_bitcast_fusion
  578.2 53.1 %psum.7 = f32[512]{0:T(512)S(1)} all-reduce(f32[512]{0:T(512)S(1)} %get-tuple-element.44), channel_id=1, replica_groups=mesh['seq'=32,'tp'=8] {'seq'}, use_global_device_ids=true, to_apply=%region_1.2 | all-reduce | flops 512 | bytes 4096 | tf_op jit(solution)/shard_map/psum | solution.py:171
  632.6 67.7 %reduce-scatter.2.cloned.1.call-done = f32[128,512]{0,1:T(8,128)} async-done(((f32[4096,512]{0,1:T(8,128)}), f32[128,512]{0,1:T(8,128)}) %reduce-scatter.2.cloned.1.call-update) | async-done | bytes 262160 | tf_op jit(solution)/shard_map/reduce_scatter | solution.py:175
  (46 shorter events, 45.2 us)
Async XLA Ops:
  7.2 63.3 %all-gather.2.cloned.1.call-start = ((), (), s32[]{:S(2)}) async-start(), calls=%async_computation.5 | async-start | bytes 2359296 | tf_op jit(solution)/shard_map/all_gather | solution.py:111
  10.8 64.5 %copy-start.5 = (bf16[256,512]{1,0:T(8,128)(2,1)S(1)}, bf16[256,512]{1,0:T(8,128)(2,1)}, u32[]{:S(2)}) copy-start(bf16[256,512]{1,0:T(8,128)(2,1)} %param.7) | copy-start | bytes 786436
  74.5 0.8 copy-start.2
  78.3 48.2 %all-to-all-start = ((f32[3,1,256,512]{3,1,0,2:T(1,128)}), f32[3,1,256,512]{3,1,0,2:T(1,128)S(1)}, u32[]{:S(2)}, u32[]{:S(2)}) async-start(f32[3,1,256,512]{3,1,0,2:T(1,128)} %copy.66), calls=%async_computation | async-start | bytes 3145728 | tf_op jit(solution)/shard_map/all_to_all | solution.py:139
  143.5 145.7 %all-to-all-start.1 = ((f32[2,3,64,1,8,512]{5,4,1,0,3,2:T(8,128)}), f32[2,3,64,1,8,512]{5,4,1,0,3,2:T(8,128)}, u32[]{:S(2)}, u32[]{:S(2)}) async-start(f32[2,3,64,1,8,512]{5,4,1,0,3,2:T(8,128)} %copy.70), calls=%async_computation.1 | async-start | bytes 12582912 | tf_op jit(solution)/shard_map/all_to_all | solution.py:146
  148.4 551.8 %reduce-scatter.2.cloned.1.call-start = ((), (), s32[]{:S(2)}) async-start(), calls=%async_computation.6 | async-start | bytes 8650752 | tf_op jit(solution)/shard_map/reduce_scatter | solution.py:175
  508.7 5.2 copy-start
  525.5 45.8 %copy-start.4 = (bf16[256,4096]{1,0:T(8,128)(2,1)S(1)}, bf16[256,4096]{1,0:T(8,128)(2,1)}, u32[]{:S(2)}) copy-start(bf16[256,4096]{1,0:T(8,128)(2,1)} %all-gather.2.cloned.1.call-done) | copy-start | bytes 6291460
  575.9 1.0 copy-start.1
  575.9 1.2 copy-start.3
Sparse Core Ops, SparseCore 0:
  10.5 59.9 all-gather.1
  576.0 124.1 reduce-scatter.1
where the time goes:
time: 713 us; the launch traced here: 709 us
  waiting for transfers between devices  308 us (43%)
  blocking collectives  246 us (35%)
  matrix products  68.1 us (10%)
  local copies, waits for them, and re-layouts  48.6 us (7%)
  between operations  14.5 us (2%)
  starting transfers between devices  14.1 us (2%)
  other arithmetic  10.2 us (1%)
    all_to_all x1, blocking collectives, on_device(): lax.all_to_all(inverted[:, :, None], 'seq', split_axis=4, concat_axis=2,...  148 us
    all_to_all x1, waiting for transfers between devices, on_device(): lax.all_to_all(half_spectrum[:, :, :, None], 'seq', split_axis=2, concat_...  141 us
    reduce_scatter x1, waiting for transfers between devices, on_device(): lax.psum_scatter(term * norm_scale, 'seq', scatter_dimension=0, tiled=True)  67.7 us
    all_gather x1, waiting for transfers between devices, on_device(): full_grad = lax.all_gather(out_grad, 'tp', axis=1, tiled=True)  59.6 us
    psum x1, blocking collectives, on_device(): decay_grad = -norm_scale * lax.psum(decay_part, 'seq')  53.1 us
    all_to_all x1, blocking collectives, on_device(): lax.all_to_all(fields_away, 'seq', split_axis=1, concat_axis=2, tiled=True)  44.9 us
    all_to_all x1, waiting for transfers between devices, on_device(): lax.all_to_all(fields, 'seq', split_axis=2, concat_axis=1, tiled=True)  38.9 us
  transfers between devices with their start and end apart: 4, of which 4 were waited for; matrix products, arithmetic and copies ran while one was open for 1% of the time, Pallas kernels for 0%

commit v1 on v0

--- a/solution.py
+++ b/solution.py
@@ -108,7 +108,10 @@
     length = tok_rows * seq_parts
     padded = 2 * length
     norm_scale = 1.0 / math.sqrt(length)
-    full_grad = lax.all_gather(out_grad, "tp", axis=1, tiled=True)
+    peers = lax.axis_size("tp")
+    shards = jnp.stack([out_grad for _ in range(peers)])
+    shards = lax.all_to_all(shards, "tp", split_axis=0, concat_axis=0)
+    full_grad = jnp.concatenate(shards, axis=1)
     grad_y = jnp.dot(full_grad, out_weight, preferred_element_type=jnp.float32).astype(jnp.bfloat16)
     outer_cos, outer_sin = angles(
         jnp.arange(2 * seq_parts, dtype=jnp.int32),

time: 713 us -> 686 us (0.962)
  waiting for transfers between devices: 308 us -> 272 us
  starting transfers between devices: 14.1 us -> 22 us
    all_gather x1 -> x0, waiting for transfers between devices: 59.6 us -> none  [on_device(): full_grad = lax.all_gather(out_grad, 'tp', axis=1, tiled=True)]
    all_to_all x0 -> x1, waiting for transfers between devices: none -> 25.7 us  [on_device(): shards = lax.all_to_all(shards, 'tp', split_axis=0, concat_axis=0)]
    all_to_all x0 -> x1, starting transfers between devices: none -> 7.43 us  [on_device(): shards = lax.all_to_all(shards, 'tp', split_axis=0, concat_axis=0)]
  transfers between devices with their start and end apart: 4 -> 4, of which waited for: 4 -> 4; matrix products, arithmetic and copies ran while one was open for 1% -> 0% of each run, Pallas kernels for 0% -> 0%
where the time goes in v1:
time: 686 us; the launch traced here: 682 us
  waiting for transfers between devices  272 us (40%)
  blocking collectives  246 us (36%)
  matrix products  68.2 us (10%)
  local copies, waits for them, and re-layouts  50.8 us (7%)
  starting transfers between devices  22 us (3%)
  between operations  14.6 us (2%)
  other arithmetic  7.54 us (1%)
    all_to_all x1, blocking collectives, on_device(): lax.all_to_all(inverted[:, :, None], 'seq', split_axis=4, concat_axis=2,...  148 us
    all_to_all x1, waiting for transfers between devices, on_device(): lax.all_to_all(half_spectrum[:, :, :, None], 'seq', split_axis=2, concat_...  141 us
    reduce_scatter x1, waiting for transfers between devices, on_device(): lax.psum_scatter(term * norm_scale, 'seq', scatter_dimension=0, tiled=True)  67.3 us
    psum x1, blocking collectives, on_device(): decay_grad = -norm_scale * lax.psum(decay_part, 'seq')  53 us
    all_to_all x1, blocking collectives, on_device(): lax.all_to_all(fields_away, 'seq', split_axis=1, concat_axis=2, tiled=True)  44.9 us
    all_to_all x1, waiting for transfers between devices, on_device(): lax.all_to_all(fields, 'seq', split_axis=2, concat_axis=1, tiled=True)  38.9 us
    all_to_all x1, waiting for transfers between devices, on_device(): shards = lax.all_to_all(shards, 'tp', split_axis=0, concat_axis=0)  25.7 us
  transfers between devices with their start and end apart: 4, of which 4 were waited for; matrix products, arithmetic and copies ran while one was open for 0% of the time, Pallas kernels for 0%

profile of v1, /device:TPU:4, one launch (start us, length us, event | category | flops | bytes accessed | tf_op | source)
XLA Modules:
  0.0 681.7 jit_solution(5480945717035879626)
XLA Ops:
  9.8 7.4 %all-to-all-start = ((bf16[8,256,512]{1,2,0:T(8,128)(2,1)}), bf16[8,256,512]{1,2,0:T(8,128)(2,1)S(1)}, u32[]{:S(2)}, u32[]{:S(2)}) async-start(bf16[8,256,512]{1,2,0:T(8,128)(2,1)} %stack.65), calls=%async_computation | async-start | bytes 4194304 | tf_op jit(solution)/shard_map/all_to_all | solution.py:113
  17.3 25.7 %all-to-all-done = bf16[8,256,512]{1,2,0:T(8,128)(2,1)S(1)} async-done(((bf16[8,256,512]{1,2,0:T(8,128)(2,1)}), bf16[8,256,512]{1,2,0:T(8,128)(2,1)S(1)}, u32[]{:S(2)}, u32[]{:S(2)}) %all-to-all-start) | async-done | bytes 2097184 | tf_op jit(solution)/shard_map/all_to_all | solution.py:113
  43.0 4.2 fusion.30
  50.9 9.7 %all-to-all-start.1 = ((f32[3,1,256,512]{3,1,0,2:T(1,128)}), f32[3,1,256,512]{3,1,0,2:T(1,128)S(1)}, u32[]{:S(2)}, u32[]{:S(2)}) async-start(f32[3,1,256,512]{3,1,0,2:T(1,128)} %copy.70), calls=%async_computation.1 | async-start | bytes 3145728 | tf_op jit(solution)/shard_map/all_to_all | solution.py:142
  60.7 38.9 %all-to-all-done.1 = f32[3,1,256,512]{3,1,0,2:T(1,128)S(1)} async-done(((f32[3,1,256,512]{3,1,0,2:T(1,128)}), f32[3,1,256,512]{3,1,0,2:T(1,128)S(1)}, u32[]{:S(2)}, u32[]{:S(2)}) %all-to-all-start.1) | async-done | bytes 1572896 | tf_op jit(solution)/shard_map/all_to_all | solution.py:142
  103.8 5.0 fusion.9
  110.0 6.7 copy.74
  116.7 4.9 all-to-all-start.2
  121.8 140.6 %all-to-all-done.2 = f32[2,3,64,1,8,512]{5,4,1,0,3,2:T(8,128)} async-done(((f32[2,3,64,1,8,512]{5,4,1,0,3,2:T(8,128)}), f32[2,3,64,1,8,512]{5,4,1,0,3,2:T(8,128)}, u32[]{:S(2)}, u32[]{:S(2)}) %all-to-all-start.2) | async-done | bytes 6291488 | tf_op jit(solution)/shard_map/all_to_all | solution.py:149
  267.2 6.3 fusion.2
  273.5 6.5 fusion
  280.0 6.4 add_bitcast_fusion.1
  286.4 6.7 subtract_bitcast_fusion.1
  301.4 4.3 fusion.24
  305.8 4.3 subtract_bitcast_fusion
  313.1 10.3 %copy.82 = f32[2,3,1,2,256,512]{5,3,1,0,2,4:T(2,128)} copy(f32[2,3,1,2,256,512]{4,5,3,1,0,2:T(8,128)} %maximum_bitcast_fusion.1) | data formatting | bytes 12582912 | tf_op jit(solution)/shard_map/broadcast_in_dim | solution.py:157
  323.4 148.1 %all_to_all.56 = f32[2,3,1,2,256,512]{5,3,1,0,2,4:T(2,128)S(1)} all-to-all(f32[2,3,1,2,256,512]{5,3,1,0,2,4:T(2,128)} %copy.82), channel_id=1, replica_groups=mesh['seq'=32,'tp'=8] {'seq'}, dimensions={4} | all-to-all | bytes 12582912 | tf_op jit(solution)/shard_map/all_to_all | solution.py:157
  481.7 5.2 fusion.67
  486.9 4.1 copy.85
  491.0 4.1 squeeze.28
  499.5 44.9 %all_to_all.57 = f32[3,32,8,512]{3,2,0,1:T(8,128)S(1)} all-to-all(f32[3,32,8,512]{3,2,0,1:T(8,128)S(1)} %copy.86), channel_id=1, replica_groups=mesh['seq'=32,'tp'=8] {'seq'}, dimensions={1} | all-to-all | bytes 3145728 | tf_op jit(solution)/shard_map/all_to_all | solution.py:162
  544.4 4.6 multiply_bitcast_fusion
  551.3 53.0 %psum.7 = f32[512]{0:T(512)S(1)} all-reduce(f32[512]{0:T(512)S(1)} %get-tuple-element.44), channel_id=1, replica_groups=mesh['seq'=32,'tp'=8] {'seq'}, use_global_device_ids=true, to_apply=%region_1.2 | all-reduce | flops 512 | bytes 4096 | tf_op jit(solution)/shard_map/psum | solution.py:174
  605.6 67.3 %reduce-scatter.2.cloned.1.call-done = f32[128,512]{0,1:T(8,128)} async-done(((f32[4096,512]{0,1:T(8,128)}), f32[128,512]{0,1:T(8,128)}) %reduce-scatter.2.cloned.1.call-update) | async-done | bytes 262160 | tf_op jit(solution)/shard_map/reduce_scatter | solution.py:178
  (54 shorter events, 48.1 us)
Async XLA Ops:
  8.3 8.9 %copy-start.9 = (f32[512]{0:T(512)S(1)}, f32[512]{0:T(512)}, u32[]{:S(2)}) copy-start(f32[512]{0:T(512)} %param.11) | copy-start | bytes 6148
  8.3 8.9 %copy-start.8 = (bf16[256,512]{1,0:T(8,128)(2,1)S(1)}, bf16[256,512]{1,0:T(8,128)(2,1)}, u32[]{:S(2)}) copy-start(bf16[256,512]{1,0:T(8,128)(2,1)} %param.6) | copy-start | bytes 786436
  9.8 33.2 %all-to-all-start = ((bf16[8,256,512]{1,2,0:T(8,128)(2,1)}), bf16[8,256,512]{1,2,0:T(8,128)(2,1)S(1)}, u32[]{:S(2)}, u32[]{:S(2)}) async-start(bf16[8,256,512]{1,2,0:T(8,128)(2,1)} %stack.65), calls=%async_computation | async-start | bytes 4194304 | tf_op jit(solution)/shard_map/all_to_all | solution.py:113
  43.0 4.2 copy-start.1
  43.0 4.2 copy-start.3
  43.0 4.3 copy-start.7
  47.2 0.8 copy-start.5
  50.9 48.7 %all-to-all-start.1 = ((f32[3,1,256,512]{3,1,0,2:T(1,128)}), f32[3,1,256,512]{3,1,0,2:T(1,128)S(1)}, u32[]{:S(2)}, u32[]{:S(2)}) async-start(f32[3,1,256,512]{3,1,0,2:T(1,128)} %copy.70), calls=%async_computation.1 | async-start | bytes 3145728 | tf_op jit(solution)/shard_map/all_to_all | solution.py:142
  116.7 145.7 %all-to-all-start.2 = ((f32[2,3,64,1,8,512]{5,4,1,0,3,2:T(8,128)}), f32[2,3,64,1,8,512]{5,4,1,0,3,2:T(8,128)}, u32[]{:S(2)}, u32[]{:S(2)}) async-start(f32[2,3,64,1,8,512]{5,4,1,0,3,2:T(8,128)} %copy.74), calls=%async_computation.2 | async-start | bytes 12582912 | tf_op jit(solution)/shard_map/all_to_all | solution.py:149
  121.6 551.3 %reduce-scatter.2.cloned.1.call-start = ((), (), s32[]{:S(2)}) async-start(), calls=%async_computation.6 | async-start | bytes 8650752 | tf_op jit(solution)/shard_map/reduce_scatter | solution.py:178
  481.7 5.2 copy-start
  498.6 45.8 %copy-start.2 = (bf16[8,256,512]{1,2,0:T(8,128)(2,1)S(1)}, bf16[8,256,512]{1,2,0:T(8,128)(2,1)}, u32[]{:S(2)}) copy-start(bf16[8,256,512]{1,2,0:T(8,128)(2,1)} %copy-done.1) | copy-start | bytes 6291460
  548.9 1.0 copy-start.4
  548.9 1.2 copy-start.6
Sparse Core Ops, SparseCore 0:
  549.1 123.7 reduce-scatter.1
